TPU v7x, 512 devices: a whole 4x8x8 slice. The times are simulated.
512 devices in a mesh: rep: 4 (over x), ep: 128 (over z, y, core).
Axes of the slice: x: 4, y: 8, z: 8, core: 2. Of those that a mesh axis runs over, the one named last changes fastest.
Arguments:
- tokens: bfloat16 [16384, 2048], P('ep', 'rep'), may hold values from -6 to 6
- out_grad: bfloat16 [16384, 2048], P('ep', 'rep'), may hold values from -6 to 6
- expert_ids: int32 [16384, 8], P('ep'), may hold values from 0 to 127, all different within a row; in each aligned block of 128 rows (0 to 127, 128 to 255, ...) at most 9 rows name the same one
- route_weight: bfloat16 [16384, 8], P('ep'), may hold values from 0.019897461 to 0.29882812
- w_gate: bfloat16 [128, 2048, 640], P('ep', 'rep'), may hold values from -0.125 to 0.125
- w_up: bfloat16 [128, 2048, 640], P('ep', 'rep'), may hold values from -0.125 to 0.125
- w_down: bfloat16 [128, 640, 2048], P('ep', None, 'rep'), may hold values from -0.25 to 0.25
Outputs:
- token_grad: bfloat16 [16384, 2048], P('ep', 'rep')
- grad_gate: bfloat16 [128, 2048, 640], P('ep', 'rep')
- grad_up: bfloat16 [128, 2048, 640], P('ep', 'rep')
- grad_down: bfloat16 [128, 640, 2048], P('ep', None, 'rep')
Inputs may be any that keep to these rules, and one draw needn't show every extreme that they name: `expert_ids`: each token picks 8 different experts. Among the 128 tokens of one index of ep no expert is picked by more than 9 tokens, and in every draw some expert is picked by exactly 9 tokens of some such index.
All inputs are finite; a program needn't handle non-finite values.
Results may differ from a plain program's by a relative error of at most 0.024.
Values may be sent and summed in bfloat16 or wider, within the bound.
No kernel may reach another device: no remote copies, remote signals or barrier semaphores. Data moves between devices by JAX's collectives and lax.ppermute only.
A program may use at most 64 MiB of HBM per device.

v0:
```python
import jax
import jax.numpy as jnp
from jax import lax
from jax.sharding import PartitionSpec as P

CAP = 9


def hidden_terms(pre_gate, pre_up, pre_back, weight):
    sigmoid_gate = jax.nn.sigmoid(pre_gate)
    silu_gate = pre_gate * sigmoid_gate
    d_hidden = weight[..., None] * pre_back
    hidden = (silu_gate * pre_up).astype(jnp.bfloat16)
    gate_delta = (
        d_hidden * pre_up * sigmoid_gate * (1.0 + pre_gate * (1.0 - sigmoid_gate))
    ).astype(jnp.bfloat16)
    up_delta = (d_hidden * silu_gate).astype(jnp.bfloat16)
    return (hidden, gate_delta, up_delta)


def body(tokens, out_grad, expert_ids, route_weight, w_gate, w_up, w_down):
    ep_ranks = lax.axis_size("ep")
    local_count = w_gate.shape[0]
    experts = local_count * ep_ranks
    quarter = tokens.shape[1]
    slot_rows = ep_ranks * CAP
    slot_total = experts * CAP
    expert_range = jnp.arange(experts, dtype=jnp.int32)
    matches = expert_ids[:, :, None] == expert_range[None, None, :]
    picked = jnp.sum(matches.astype(jnp.int32), axis=1)
    before = jnp.cumsum(picked, axis=0) - picked
    position = jnp.sum(jnp.where(matches, before[:, None, :], 0), axis=2)
    owner_col = expert_ids // local_count
    within = expert_ids % local_count
    slot_index = (within * ep_ranks + owner_col) * CAP + position
    select = slot_index[:, :, None] == jnp.arange(slot_total, dtype=jnp.int32)[None, None, :]
    placing = jnp.any(select, axis=1).astype(jnp.bfloat16)
    send_tokens = jnp.einsum("ts,td->sd", placing, tokens, preferred_element_type=jnp.float32)
    send_tokens = send_tokens.astype(jnp.bfloat16).reshape(local_count, ep_ranks, CAP, quarter)
    send_grads = jnp.einsum("ts,td->sd", placing, out_grad, preferred_element_type=jnp.float32)
    send_grads = send_grads.astype(jnp.bfloat16).reshape(local_count, ep_ranks, CAP, quarter)
    send_weight = jnp.sum(
        jnp.where(select, route_weight.astype(jnp.float32)[:, :, None], 0.0), axis=(0, 1)
    )
    send_weight = send_weight.astype(jnp.bfloat16).reshape(local_count, ep_ranks, CAP)
    routed_tokens, routed_grads, routed_weight = (
        lax.all_to_all(send_tokens, "ep", split_axis=1, concat_axis=1, tiled=True),
        lax.all_to_all(send_grads, "ep", split_axis=1, concat_axis=1, tiled=True),
        lax.all_to_all(send_weight, "ep", split_axis=1, concat_axis=1, tiled=True),
    )
    routed_tokens = routed_tokens.reshape(local_count, slot_rows, quarter)
    part_gate = jnp.einsum(
        "erd,edf->erf", routed_tokens, w_gate, preferred_element_type=jnp.float32
    )
    part_up = jnp.einsum("erd,edf->erf", routed_tokens, w_up, preferred_element_type=jnp.float32)
    routed_grads = routed_grads.reshape(local_count, slot_rows, quarter)
    part_back = jnp.einsum("erd,efd->erf", routed_grads, w_down, preferred_element_type=jnp.float32)
    weight = routed_weight.reshape(local_count, slot_rows).astype(jnp.float32)
    pre_gate, pre_up, pre_back = (
        lax.psum(part_gate.astype(jnp.bfloat16), "rep").astype(jnp.float32),
        lax.psum(part_up.astype(jnp.bfloat16), "rep").astype(jnp.float32),
        lax.psum(part_back.astype(jnp.bfloat16), "rep").astype(jnp.float32),
    )
    hidden, gate_delta, up_delta = hidden_terms(pre_gate, pre_up, pre_back, weight)
    scaled_grad = (weight[:, :, None] * routed_grads.astype(jnp.float32)).astype(jnp.bfloat16)
    back_rows = jnp.einsum("erf,edf->erd", gate_delta, w_gate, preferred_element_type=jnp.float32)
    back_rows = back_rows + jnp.einsum(
        "erf,edf->erd", up_delta, w_up, preferred_element_type=jnp.float32
    )
    back_rows = back_rows.astype(jnp.bfloat16).reshape(local_count, ep_ranks, CAP, quarter)
    returned = lax.all_to_all(back_rows, "ep", split_axis=1, concat_axis=1, tiled=True)
    grad_gate = jnp.einsum(
        "erd,erf->edf", routed_tokens, gate_delta, preferred_element_type=jnp.float32
    ).astype(jnp.bfloat16)
    grad_up = jnp.einsum(
        "erd,erf->edf", routed_tokens, up_delta, preferred_element_type=jnp.float32
    ).astype(jnp.bfloat16)
    grad_down = jnp.einsum(
        "erf,erd->efd", hidden, scaled_grad, preferred_element_type=jnp.float32
    ).astype(jnp.bfloat16)
    token_grad = jnp.einsum(
        "ts,sd->td",
        placing,
        returned.reshape(slot_total, quarter),
        preferred_element_type=jnp.float32,
    )
    return (token_grad.astype(jnp.bfloat16), grad_gate, grad_up, grad_down)


def solution(mesh):
    placed = (
        P("ep", "rep"),
        P("ep", "rep"),
        P("ep", None),
        P("ep", None),
        P("ep", "rep", None),
        P("ep", "rep", None),
        P("ep", None, "rep"),
    )
    return jax.shard_map(
        body,
        mesh=mesh,
        in_specs=placed,
        out_specs=(
            P("ep", "rep"),
            P("ep", "rep", None),
            P("ep", "rep", None),
            P("ep", None, "rep"),
        ),
        check_vma=False,
    )
```

profile of v0, /device:TPU:8, one launch (start us, length us, event | category | flops | bytes accessed | tf_op | source)
XLA Modules:
  0.0 345.2 jit_solution(13522083225533455690)
XLA Ops:
  7.2 0.0 copy-start
  7.2 0.9 copy.35
  8.0 0.2 convert_reduce_fusion
  8.3 0.2 reduce_window_sum.11
  8.4 2.4 select_reduce_fusion.1
  10.9 0.7 multiply_add_fusion
  11.6 0.1 copy.37
  11.7 0.6 copy-done.11
  12.3 1.5 fusion
  13.8 1.4 convolution_convert_fusion.3
  15.2 1.6 reshape.170
  16.8 17.5 %all-to-all-start.2 = ((bf16[1,128,9,512]{3,2,0,1:T(8,128)(2,1)}), bf16[1,128,9,512]{3,2,0,1:T(8,128)(2,1)S(1)}, u32[]{:S(2)}, u32[]{:S(2)}) async-start(bf16[1,128,9,512]{3,2,0,1:T(8,128)(2,1)} %bitcast.72), calls=%async_computation.2 | async-start | bytes 4194304 | tf_op jit(solution)/shard_map/all_to_all | solution.py:47
  34.3 1.5 convolution_convert_fusion.4
  35.8 3.3 reshape.167
  39.1 49.2 %all-to-all-done.2 = bf16[1,128,9,512]{3,2,0,1:T(8,128)(2,1)S(1)} async-done(((bf16[1,128,9,512]{3,2,0,1:T(8,128)(2,1)}), bf16[1,128,9,512]{3,2,0,1:T(8,128)(2,1)S(1)}, u32[]{:S(2)}, u32[]{:S(2)}) %all-to-all-start.2) | async-done | bytes 1179680 | tf_op jit(solution)/shard_map/all_to_all | solution.py:47
  88.4 1.3 copy-done.1
  89.7 6.1 %all-to-all-start.1 = ((bf16[1,128,9,512]{3,2,0,1:T(8,128)(2,1)}), bf16[1,128,9,512]{3,2,0,1:T(8,128)(2,1)S(1)}, u32[]{:S(2)}, u32[]{:S(2)}) async-start(bf16[1,128,9,512]{3,2,0,1:T(8,128)(2,1)} %bitcast.71), calls=%async_computation.1 | async-start | bytes 4194304 | tf_op jit(solution)/shard_map/all_to_all | solution.py:48
  95.7 0.0 copy-start.10
  95.7 0.2 all-reduce.3.cloned.1.call-start
  96.0 3.6 %reshape.171 = bf16[1152,512]{1,0:T(8,128)(2,1)} reshape(bf16[1,128,9,512]{3,2,0,1:T(8,128)(2,1)} %copy-done.1) | data formatting | bytes 2359296 | tf_op jit(solution)/shard_map/reshape.4
  99.6 3.6 %fusion.11 = bf16[1,1152,640]{2,1,0:T(8,128)(2,1)} fusion(bf16[1152,512]{1,0:T(8,128)(2,1)} %reshape.171, bf16[1,512,640]{2,1,0:T(8,128)(2,1)S(1)} %copy-done.10), kind=kOutput, calls=%fused_computation.26 | convolution fusion | flops 755712000 | bytes 3309568 | tf_op jit(solution)/shard_map/erd,edf->erf/dot_general | solution.py:55
  103.2 2.2 fusion.12
  105.4 44.4 %all-to-all-done.1 = bf16[1,128,9,512]{3,2,0,1:T(8,128)(2,1)S(1)} async-done(((bf16[1,128,9,512]{3,2,0,1:T(8,128)(2,1)}), bf16[1,128,9,512]{3,2,0,1:T(8,128)(2,1)S(1)}, u32[]{:S(2)}, u32[]{:S(2)}) %all-to-all-start.1) | async-done | bytes 1179680 | tf_op jit(solution)/shard_map/all_to_all | solution.py:48
  149.8 1.3 reshape.168
  151.1 3.7 %fusion.10 = bf16[1,1152,640]{2,1,0:T(8,128)(2,1)} fusion(bf16[1152,512]{1,0:T(8,128)(2,1)} %reshape.168, bf16[1,640,512]{2,1,0:T(8,128)(2,1)} %param.13), kind=kOutput, calls=%fused_computation.25 | convolution fusion | flops 755712000 | bytes 3309568 | tf_op jit(solution)/shard_map/erd,efd->erf/dot_general | solution.py:57
  154.9 0.0 all-reduce.3.cloned.1.call-update
  154.9 1.4 copy.38
  156.3 2.1 select_reduce_fusion
  158.4 1.6 convert_element_type.176
  159.9 16.8 %all_to_all.20 = bf16[1,128,9]{2,0,1:T(2,128)(2,1)S(1)} all-to-all(bf16[1,128,9]{2,0,1:T(2,128)(2,1)} %convert_element_type.176), channel_id=1, replica_groups=mesh['rep'=4,'ep'=128] {'ep'}, dimensions={1} | all-to-all | bytes 4608 | tf_op jit(solution)/shard_map/all_to_all | solution.py:49
  176.7 0.8 convert_reduce_fusion.1
  177.5 1.6 reshape.179
  179.2 76.7 %all-reduce.3.cloned.1.call-done = (bf16[1,1152,640]{2,1,0:T(8,128)(2,1)}, bf16[1,1152,640]{2,1,0:T(8,128)(2,1)}, bf16[1,1152,640]{2,1,0:T(8,128)(2,1)}) async-done(((bf16[1,1152,640]{2,1,0:T(8,128)(2,1)}, bf16[1,1152,640]{2,1,0:T(8,128)(2,1)}, bf16[1,1152,640]{2,1,0:T(8,128)(2,1)}), (bf16[1,1152,640]{2,1,0:T(8,128)(2,1)}, bf16[1,1152,640]{2,1,0:T(8,128)(2,1)}, ...) | async-done | bytes 4423696 | tf_op jit(solution)/shard_map/psum | solution.py:61
  255.9 3.5 %fusion.13 = (bf16[1152,640]{1,0:T(8,128)(2,1)S(1)}, bf16[1,1152,640]{2,1,0:T(8,128)(2,1)S(1)}) fusion(bf16[1,1152,640]{2,1,0:T(8,128)(2,1)} %get-tuple-element.6, f32[1152]{0:T(1024)} %reshape.179, bf16[1,1152,640]{2,1,0:T(8,128)(2,1)} %get-tuple-element.5, bf16[1,1152,640]{2,1,0:T(8,128)(2,1)} %get-tuple-element.4), kind=kLoop, calls=%fused_computation.29 | loop fusion | flops 12533760 | bytes 7377408 | tf_op jit(solution)/shard_map/reshape.25
  259.4 1.1 fusion.19
  260.5 0.4 copy-done.2
  260.9 2.2 fusion.1
  263.1 3.3 reshape.176
  266.4 14.6 %all-to-all-start.3 = ((bf16[1,128,9,512]{3,2,0,1:T(8,128)(2,1)}), bf16[1,128,9,512]{3,2,0,1:T(8,128)(2,1)}, u32[]{:S(2)}, u32[]{:S(2)}) async-start(bf16[1,128,9,512]{3,2,0,1:T(8,128)(2,1)} %bitcast.70), calls=%async_computation.3 | async-start | bytes 4194304 | tf_op jit(solution)/shard_map/all_to_all | solution.py:71
  281.1 0.0 copy-start.13
  281.1 4.2 %reshape.180 = f32[1,1152,1,1,1,1,512]{6,0,1,5,4,3,2:T(1,128)} reshape(bf16[1,128,9,512]{3,2,0,1:T(8,128)(2,1)S(1)} %all-to-all-done.1) | data formatting | bytes 3538944 | tf_op jit(solution)/shard_map/convert_element_type | solution.py:65
  285.3 5.4 %multiply_convert_fusion.1 = bf16[1,1152,1,1,1,1,512]{6,0,1,5,4,3,2:T(2,128)(2,1)S(1)} fusion(f32[1,1152,1,1,1,1,512]{6,0,1,5,4,3,2:T(1,128)} %reshape.180, f32[1152]{0:T(1024)S(1)} %copy-done.13), kind=kLoop, calls=%fused_computation.28 | loop fusion | flops 1179648 | bytes 3543552 | tf_op jit(solution)/shard_map/convert_element_type | solution.py:65
  290.7 2.0 fusion.27
  292.8 2.0 fusion.28
  294.8 2.2 fusion.31
  297.1 37.7 %all-to-all-done.3 = bf16[1,128,9,512]{3,2,0,1:T(8,128)(2,1)} async-done(((bf16[1,128,9,512]{3,2,0,1:T(8,128)(2,1)}), bf16[1,128,9,512]{3,2,0,1:T(8,128)(2,1)}, u32[]{:S(2)}, u32[]{:S(2)}) %all-to-all-start.3) | async-done | bytes 1179680 | tf_op jit(solution)/shard_map/all_to_all | solution.py:71
  334.8 2.5 reshape.177
  337.3 1.0 convolution_convert_fusion.6
  (24 shorter events, 0.1 us)
Async XLA Ops:
  7.2 96.0 %copy-start = (bf16[1,512,640]{2,1,0:T(8,128)(2,1)S(1)}, bf16[1,512,640]{2,1,0:T(8,128)(2,1)}, u32[]{:S(2)}) copy-start(bf16[1,512,640]{2,1,0:T(8,128)(2,1)} %param.11) | copy-start | bytes 1966084
  11.7 0.6 copy-start.11
  16.8 17.5 %copy-start.12 = (bf16[128,512]{1,0:T(8,128)(2,1)S(1)}, bf16[128,512]{1,0:T(8,128)(2,1)}, u32[]{:S(2)}) copy-start(bf16[128,512]{1,0:T(8,128)(2,1)} %param.8) | copy-start | bytes 393220
  16.8 71.6 %all-to-all-start.2 = ((bf16[1,128,9,512]{3,2,0,1:T(8,128)(2,1)}), bf16[1,128,9,512]{3,2,0,1:T(8,128)(2,1)S(1)}, u32[]{:S(2)}, u32[]{:S(2)}) async-start(bf16[1,128,9,512]{3,2,0,1:T(8,128)(2,1)} %bitcast.72), calls=%async_computation.2 | async-start | bytes 4194304 | tf_op jit(solution)/shard_map/all_to_all | solution.py:47
  88.4 1.3 copy-start.1
  89.7 60.1 %all-to-all-start.1 = ((bf16[1,128,9,512]{3,2,0,1:T(8,128)(2,1)}), bf16[1,128,9,512]{3,2,0,1:T(8,128)(2,1)S(1)}, u32[]{:S(2)}, u32[]{:S(2)}) async-start(bf16[1,128,9,512]{3,2,0,1:T(8,128)(2,1)} %bitcast.71), calls=%async_computation.1 | async-start | bytes 4194304 | tf_op jit(solution)/shard_map/all_to_all | solution.py:48
  95.7 3.8 %copy-start.10 = (bf16[1,512,640]{2,1,0:T(8,128)(2,1)S(1)}, bf16[1,512,640]{2,1,0:T(8,128)(2,1)}, u32[]{:S(2)}) copy-start(bf16[1,512,640]{2,1,0:T(8,128)(2,1)} %param.12) | copy-start | bytes 1966084
  95.7 160.1 %all-reduce.3.cloned.1.call-start = ((), (), s32[]{:S(2)}) async-start(), calls=%async_computation.4 | async-start | bytes 8847360 | tf_op jit(solution)/shard_map/psum | solution.py:61
  99.6 3.6 %copy-start.8 = (bf16[1152,512]{1,0:T(8,128)(2,1)S(1)}, bf16[1152,512]{1,0:T(8,128)(2,1)}, u32[]{:S(2)}) copy-start(bf16[1152,512]{1,0:T(8,128)(2,1)} %reshape.171) | copy-start | bytes 3538948
  259.4 1.1 copy-start.6
  259.4 1.6 copy-start.2
  266.4 68.3 %all-to-all-start.3 = ((bf16[1,128,9,512]{3,2,0,1:T(8,128)(2,1)}), bf16[1,128,9,512]{3,2,0,1:T(8,128)(2,1)}, u32[]{:S(2)}, u32[]{:S(2)}) async-start(bf16[1,128,9,512]{3,2,0,1:T(8,128)(2,1)} %bitcast.70), calls=%async_computation.3 | async-start | bytes 4194304 | tf_op jit(solution)/shard_map/all_to_all | solution.py:71
  281.1 4.3 %copy-start.13 = (f32[1152]{0:T(1024)S(1)}, f32[1152]{0:T(1024)}, u32[]{:S(2)}) copy-start(f32[1152]{0:T(1024)} %reshape.179) | copy-start | bytes 13828
  285.3 5.4 %copy-start.3 = (bf16[1152,640]{1,0:T(8,128)(2,1)S(1)}, bf16[1152,640]{1,0:T(8,128)(2,1)}, u32[]{:S(2)}) copy-start(bf16[1152,640]{1,0:T(8,128)(2,1)} %copy-done.2) | copy-start | bytes 4423684
  285.3 5.4 %copy-start.9 = (bf16[1152,512]{1,0:T(8,128)(2,1)S(1)}, bf16[1152,512]{1,0:T(8,128)(2,1)}, u32[]{:S(2)}) copy-start(bf16[1152,512]{1,0:T(8,128)(2,1)} %reshape.171) | copy-start | bytes 3538948
  290.7 2.1 copy-start.7
  292.8 2.1 copy-start.4
  292.8 2.1 copy-start.5
Sparse Core Ops, SparseCore 0:
  155.0 100.8 all-reduce.2
where the time goes:
time: 346 us; the launch traced here: 345 us
  waiting for transfers between devices  208 us (60%)
  starting transfers between devices  38.4 us (11%)
  local copies, waits for them, and re-layouts  27.9 us (8%)
  matrix products  23.1 us (7%)
  blocking collectives  16.8 us (5%)
  other arithmetic  16.7 us (5%)
  between operations  14.2 us (4%)
    psum x1, waiting for transfers between devices, body(): lax.psum(part_up.astype(jnp.bfloat16), 'rep').astype(jnp.float32)  76.7 us
    all_to_all x1, waiting for transfers between devices, body(): lax.all_to_all(send_tokens, 'ep', split_axis=1, concat_axis=1, tiled=True)  49.2 us
    all_to_all x1, waiting for transfers between devices, body(): lax.all_to_all(send_grads, 'ep', split_axis=1, concat_axis=1, tiled=True)  44.4 us
    all_to_all x1, waiting for transfers between devices, body(): lax.all_to_all(back_rows, 'ep', split_axis=1, concat_axis=1, tiled=True)  37.7 us
    all_to_all x1, starting transfers between devices, body(): lax.all_to_all(send_tokens, 'ep', split_axis=1, concat_axis=1, tiled=True)  17.5 us
    all_to_all x1, blocking collectives, body(): lax.all_to_all(send_weight, 'ep', split_axis=1, concat_axis=1, tiled=True)  16.8 us
    all_to_all x1, starting transfers between devices, body(): lax.all_to_all(back_rows, 'ep', split_axis=1, concat_axis=1, tiled=True)  14.6 us
  transfers between devices with their start and end apart: 4, of which 4 were waited for; matrix products, arithmetic and copies ran while one was open for 11% of the time, Pallas kernels for 0%

commit v1 on v0

--- a/solution.py
+++ b/solution.py
@@ -58,7 +58,7 @@
     weight = routed_weight.reshape(local_count, slot_rows).astype(jnp.float32)
     pre_gate, pre_up, pre_back = (
         lax.psum(part_gate.astype(jnp.bfloat16), "rep").astype(jnp.float32),
-        lax.psum(part_up.astype(jnp.bfloat16), "rep").astype(jnp.float32),
+        jnp.sum(lax.all_gather(part_up.astype(jnp.bfloat16), "rep"), axis=0).astype(jnp.float32),
         lax.psum(part_back.astype(jnp.bfloat16), "rep").astype(jnp.float32),
     )
     hidden, gate_delta, up_delta = hidden_terms(pre_gate, pre_up, pre_back, weight)

time: 346 us -> 332 us (0.960)
  blocking collectives: 16.8 us -> 148 us
  waiting for transfers between devices: 208 us -> 85.5 us
  starting transfers between devices: 38.4 us -> 14.7 us
  other arithmetic: 16.7 us -> 21.8 us
    all_to_all x0 -> x2, blocking collectives: none -> 131 us  [the longest x1 71.3 us: body(): lax.all_to_all(send_tokens, 'ep', split_axis=1, concat_axis=1, tiled=True)]
    all_to_all x2 -> x0, waiting for transfers between devices: 93.6 us -> none  [the longest x1 49.2 us: body(): lax.all_to_all(send_tokens, 'ep', split_axis=1, concat_axis=1, tiled=True)]
    psum x1, waiting for transfers between devices: 76.7 us -> 47.8 us  [body(): lax.psum(part_gate.astype(jnp.bfloat16), 'rep').astype(jnp.float32)]
    all_to_all x2 -> x0, starting transfers between devices: 23.6 us -> none  [the longest x1 17.5 us: body(): lax.all_to_all(send_tokens, 'ep', split_axis=1, concat_axis=1, tiled=True)]
    reduce_sum x0 -> x1, other arithmetic: none -> 5.12 us  [body(): jnp.sum(lax.all_gather(part_up.astype(jnp.bfloat16), 'rep'), axis=0)]
  transfers between devices with their start and end apart: 4 -> 3, of which waited for: 4 -> 2; matrix products, arithmetic and copies ran while one was open for 11% -> 11% of each run, Pallas kernels for 0% -> 0%
where the time goes in v1:
time: 332 us; the launch traced here: 331 us
  blocking collectives  148 us (45%)
  waiting for transfers between devices  85.5 us (26%)
  local copies, waits for them, and re-layouts  25.1 us (8%)
  other arithmetic  21.8 us (7%)
  matrix products  21.6 us (7%)
  starting transfers between devices  14.7 us (4%)
  between operations  14.2 us (4%)
    all_to_all x1, blocking collectives, body(): lax.all_to_all(send_tokens, 'ep', split_axis=1, concat_axis=1, tiled=True)  71.3 us
    all_to_all x1, blocking collectives, body(): lax.all_to_all(send_grads, 'ep', split_axis=1, concat_axis=1, tiled=True)  60.1 us
    psum x1, waiting for transfers between devices, body(): lax.psum(part_gate.astype(jnp.bfloat16), 'rep').astype(jnp.float32)  47.8 us
    all_to_all x1, waiting for transfers between devices, body(): lax.all_to_all(back_rows, 'ep', split_axis=1, concat_axis=1, tiled=True)  37.7 us
    all_to_all x1, blocking collectives, body(): lax.all_to_all(send_weight, 'ep', split_axis=1, concat_axis=1, tiled=True)  16.9 us
    all_to_all x1, starting transfers between devices, body(): lax.all_to_all(back_rows, 'ep', split_axis=1, concat_axis=1, tiled=True)  14.6 us
  transfers between devices with their start and end apart: 3, of which 2 were waited for; matrix products, arithmetic and copies ran while one was open for 11% of the time, Pallas kernels for 0%

profile of v1, /device:TPU:8, one launch (start us, length us, event | category | flops | bytes accessed | tf_op | source)
XLA Modules:
  0.0 331.3 jit_solution(11913290822685638270)
XLA Ops:
  7.2 0.0 copy-start
  7.2 0.0 all-gather.3.cloned.1.call-start
  7.2 0.8 copy.35
  8.1 0.2 convert_reduce_fusion
  8.3 0.2 reduce_window_sum.11
  8.5 2.4 select_reduce_fusion.1
  10.9 0.7 multiply_add_fusion
  11.6 0.1 copy.37
  11.7 1.5 fusion
  13.2 0.0 copy-done.11
  13.2 2.4 convolution_convert_fusion.3
  15.7 2.3 reshape.182
  18.0 71.3 %all_to_all.20 = bf16[1,128,9,512]{3,2,0,1:T(8,128)(2,1)} all-to-all(bf16[1,128,9,512]{3,2,0,1:T(8,128)(2,1)S(1)} %bitcast.81), channel_id=1, replica_groups=mesh['rep'=4,'ep'=128] {'ep'}, dimensions={1} | all-to-all | bytes 2359296 | tf_op jit(solution)/shard_map/all_to_all | solution.py:47
  89.3 2.6 reshape.183
  92.0 2.2 convolution_convert_fusion.1
  94.2 0.0 all-gather.3.cloned.1.call-update
  94.2 0.0 all-reduce.3.cloned.1.call-start
  94.2 0.8 copy-done.12
  95.1 0.5 convolution_convert_fusion.4
  95.6 1.6 reshape.179
  97.2 60.1 %all_to_all.21 = bf16[1,128,9,512]{3,2,0,1:T(8,128)(2,1)S(1)} all-to-all(bf16[1,128,9,512]{3,2,0,1:T(8,128)(2,1)} %bitcast.82), channel_id=1, replica_groups=mesh['rep'=4,'ep'=128] {'ep'}, dimensions={1} | all-to-all | bytes 2359296 | tf_op jit(solution)/shard_map/all_to_all | solution.py:48
  157.3 1.4 reshape.180
  158.6 3.6 %fusion.11 = bf16[1,1152,640]{2,1,0:T(8,128)(2,1)} fusion(bf16[1152,512]{1,0:T(8,128)(2,1)} %copy-done.7, bf16[1,512,640]{2,1,0:T(8,128)(2,1)S(1)} %copy-done), kind=kOutput, calls=%fused_computation.26 | convolution fusion | flops 755712000 | bytes 3309568 | tf_op jit(solution)/shard_map/erd,edf->erf/dot_general | solution.py:52
  162.3 2.3 fusion.10
  164.5 0.0 all-reduce.3.cloned.1.call-update
  164.5 1.4 copy.38
  166.0 2.1 select_reduce_fusion
  168.0 1.6 convert_element_type.188
  169.6 16.9 %all_to_all.22 = bf16[1,128,9]{2,0,1:T(2,128)(2,1)S(1)} all-to-all(bf16[1,128,9]{2,0,1:T(2,128)(2,1)} %convert_element_type.188), channel_id=1, replica_groups=mesh['rep'=4,'ep'=128] {'ep'}, dimensions={1} | all-to-all | bytes 4608 | tf_op jit(solution)/shard_map/all_to_all | solution.py:49
  186.5 0.8 convert_reduce_fusion.1
  187.3 1.6 reshape.191
  188.9 5.1 %reduce.2 = bf16[1152,640]{1,0:T(8,128)(2,1)} reduce(bf16[4,1152,640]{2,1,0:T(8,128)(2,1)} %bitcast.83, bf16[]{:T(256)} %constant.36.clone.1), dimensions={0}, to_apply=%region_6.7 | reduce | flops 2211840 | bytes 7372802 | tf_op jit(solution)/shard_map/reduce_sum | solution.py:61
  194.1 47.8 %all-reduce.3.cloned.1.call-done = (bf16[1,1152,640]{2,1,0:T(8,128)(2,1)}, bf16[1,1152,640]{2,1,0:T(8,128)(2,1)}) async-done(((bf16[1,1152,640]{2,1,0:T(8,128)(2,1)}, bf16[1,1152,640]{2,1,0:T(8,128)(2,1)}), (bf16[1,1152,640]{2,1,0:T(8,128)(2,1)}, bf16[1,1152,640]{2,1,0:T(8,128)(2,1)})) %all-reduce.3.cloned.1.call-update) | async-done | bytes 2949136 | tf_op jit(solution)/shard_map/psum | solution.py:60
  241.9 3.5 %fusion.12 = (bf16[1152,640]{1,0:T(8,128)(2,1)S(1)}, bf16[1,1152,640]{2,1,0:T(8,128)(2,1)S(1)}) fusion(bf16[1,1152,640]{2,1,0:T(8,128)(2,1)} %get-tuple-element.5, f32[1152]{0:T(1024)} %reshape.191, bf16[1,1152,640]{2,1,0:T(8,128)(2,1)} %get-tuple-element.4, bf16[1152,640]{1,0:T(8,128)(2,1)} %reduce.2), kind=kLoop, calls=%fused_computation.28 | loop fusion | flops 12533760 | bytes 7377408 | tf_op jit(solution)/shard_map/reshape.25
  245.4 1.1 fusion.19
  246.5 0.6 copy-done.1
  247.1 2.2 fusion.1
  249.3 3.3 reshape.188
  252.6 14.6 %all-to-all-start.3 = ((bf16[1,128,9,512]{3,2,0,1:T(8,128)(2,1)}), bf16[1,128,9,512]{3,2,0,1:T(8,128)(2,1)}, u32[]{:S(2)}, u32[]{:S(2)}) async-start(bf16[1,128,9,512]{3,2,0,1:T(8,128)(2,1)} %bitcast.80), calls=%async_computation.3 | async-start | bytes 4194304 | tf_op jit(solution)/shard_map/all_to_all | solution.py:71
  267.2 0.0 copy-start.13
  267.2 4.3 %reshape.193 = f32[1,1152,1,1,1,1,512]{6,0,1,5,4,3,2:T(1,128)} reshape(bf16[1,128,9,512]{3,2,0,1:T(8,128)(2,1)S(1)} %all_to_all.21) | data formatting | bytes 3538944 | tf_op jit(solution)/shard_map/convert_element_type | solution.py:65
  271.5 5.4 %multiply_convert_fusion.1 = bf16[1,1152,1,1,1,1,512]{6,0,1,5,4,3,2:T(2,128)(2,1)S(1)} fusion(f32[1,1152,1,1,1,1,512]{6,0,1,5,4,3,2:T(1,128)} %reshape.193, f32[1152]{0:T(1024)S(1)} %copy-done.13), kind=kLoop, calls=%fused_computation.27 | loop fusion | flops 1179648 | bytes 3543552 | tf_op jit(solution)/shard_map/convert_element_type | solution.py:65
  276.9 2.0 fusion.28
  279.0 2.0 fusion.27
  281.0 2.2 fusion.31
  283.2 37.7 %all-to-all-done.3 = bf16[1,128,9,512]{3,2,0,1:T(8,128)(2,1)} async-done(((bf16[1,128,9,512]{3,2,0,1:T(8,128)(2,1)}), bf16[1,128,9,512]{3,2,0,1:T(8,128)(2,1)}, u32[]{:S(2)}, u32[]{:S(2)}) %all-to-all-start.3) | async-done | bytes 1179680 | tf_op jit(solution)/shard_map/all_to_all | solution.py:71
  320.9 2.5 reshape.189
  323.4 1.0 convolution_convert_fusion.6
  (28 shorter events, 0.1 us)
Async XLA Ops:
  7.2 151.5 %copy-start = (bf16[1,512,640]{2,1,0:T(8,128)(2,1)S(1)}, bf16[1,512,640]{2,1,0:T(8,128)(2,1)}, u32[]{:S(2)}) copy-start(bf16[1,512,640]{2,1,0:T(8,128)(2,1)} %param.11) | copy-start | bytes 1966084
  7.2 181.8 %all-gather.3.cloned.1.call-start = ((), (), s32[]{:S(2)}) async-start(), calls=%async_computation.4 | async-start | bytes 7372800 | tf_op jit(solution)/shard_map/all_gather | solution.py:61
  11.7 1.5 copy-start.11
  89.3 2.6 copy-start.10
  92.0 2.2 copy-start.7
  94.2 0.9 copy-start.12
  94.2 147.7 %all-reduce.3.cloned.1.call-start = ((), (), s32[]{:S(2)}) async-start(), calls=%async_computation.5 | async-start | bytes 5898240 | tf_op jit(solution)/shard_map/psum | solution.py:60
  158.6 3.6 %copy-start.9 = (bf16[1152,512]{1,0:T(8,128)(2,1)S(1)}, bf16[1152,512]{1,0:T(8,128)(2,1)}, u32[]{:S(2)}) copy-start(bf16[1152,512]{1,0:T(8,128)(2,1)} %reshape.180) | copy-start | bytes 3538948
  158.6 3.6 %copy-start.14 = (bf16[1,640,512]{2,1,0:T(8,128)(2,1)S(1)}, bf16[1,640,512]{2,1,0:T(8,128)(2,1)}, u32[]{:S(2)}) copy-start(bf16[1,640,512]{2,1,0:T(8,128)(2,1)} %param.13) | copy-start | bytes 1966084
  245.4 1.1 copy-start.5
  245.4 1.7 copy-start.1
  252.6 68.3 %all-to-all-start.3 = ((bf16[1,128,9,512]{3,2,0,1:T(8,128)(2,1)}), bf16[1,128,9,512]{3,2,0,1:T(8,128)(2,1)}, u32[]{:S(2)}, u32[]{:S(2)}) async-start(bf16[1,128,9,512]{3,2,0,1:T(8,128)(2,1)} %bitcast.80), calls=%async_computation.3 | async-start | bytes 4194304 | tf_op jit(solution)/shard_map/all_to_all | solution.py:71
  267.2 4.3 %copy-start.13 = (f32[1152]{0:T(1024)S(1)}, f32[1152]{0:T(1024)}, u32[]{:S(2)}) copy-start(f32[1152]{0:T(1024)} %reshape.191) | copy-start | bytes 13828
  271.5 5.4 %copy-start.6 = (bf16[1,1152,640]{2,1,0:T(8,128)(2,1)S(1)}, bf16[1,1152,640]{2,1,0:T(8,128)(2,1)}, u32[]{:S(2)}) copy-start(bf16[1,1152,640]{2,1,0:T(8,128)(2,1)} %copy-done.5) | copy-start | bytes 4423684
  271.5 5.4 %copy-start.8 = (bf16[1152,512]{1,0:T(8,128)(2,1)S(1)}, bf16[1152,512]{1,0:T(8,128)(2,1)}, u32[]{:S(2)}) copy-start(bf16[1152,512]{1,0:T(8,128)(2,1)} %copy-done.7) | copy-start | bytes 3538948
  276.9 2.0 copy-start.2
  279.0 2.1 copy-start.3
  279.0 2.1 copy-start.4
Sparse Core Ops, SparseCore 0:
  94.3 61.0 all-gather.2
  164.7 77.1 all-reduce.2
